TPU v7x, 256 devices: a whole 4x4x8 slice. The times are simulated.
256 devices in a mesh: row: 32 (over z, x), feat: 8 (over y, core).
Axes of the slice: x: 4, y: 4, z: 8, core: 2. Of those that a mesh axis runs over, the one named last changes fastest.
Arguments:
- bin_codes: int32 [256, 262144], P(None, 'row'), may hold values from 0 to 31
- gradients: bfloat16 [262144], P('row'), may hold values from -6 to 6
- hessians: bfloat16 [262144], P('row'), may hold values from 0.019897461 to 0.25
- pair_list: int32 [64, 2], replicated, may hold values from 0 to 255, as said below
- owners: int32 [64], replicated, may hold values from 0 to 7, as said below
Outputs:
- cut_table: float32 [128, 1024], P('feat', 'row')
- best_gain: float32 [64], replicated
Inputs may be any that keep to these rules, and one draw needn't show every extreme that they name: `pair_list`: each row holds two different features, the first smaller. `owners`: one index owns exactly 16 pairs in every draw, the others at most that many.
All inputs are finite; a program needn't handle non-finite values.
Results may differ from a plain program's by a relative error of at most 0.0003.
Values sent between devices are 32-bit elements; how exact they have to be, the bound alone decides.
A program may use at most 64 MiB of HBM per device.

v0:
```python
import jax
import jax.numpy as jnp
from jax import lax
from jax.sharding import PartitionSpec as P

BINS = 32
LAMBDA_REG = 1.0


def slot_rank(owners):
    pair_ids = jnp.arange(owners.shape[0], dtype=jnp.int32)
    same_owner = owners[:, None] == owners[None, :]
    earlier = pair_ids[None, :] < pair_ids[:, None]
    return jnp.sum((same_owner & earlier).astype(jnp.int32), axis=1)


def cumulate(histogram):
    bin_count = histogram.shape[-2]
    running = jnp.cumsum(histogram, axis=-2)
    shaped = running.reshape(running.shape[:-1] + (2, bin_count))
    shaped = jnp.cumsum(shaped, axis=-1)
    return shaped.reshape(running.shape)


def cut_gains(cut_rows, margin_row):
    bin_count = margin_row.shape[-1] // 2
    grad_cum = cut_rows[..., :bin_count]
    hess_cum = cut_rows[..., bin_count:]
    grad_end = grad_cum[..., -1:]
    hess_end = hess_cum[..., -1:]
    grad_col = margin_row[..., None, :bin_count]
    hess_col = margin_row[..., None, bin_count:]
    grad_all = margin_row[..., None, bin_count - 1 : bin_count]
    hess_all = margin_row[..., None, 2 * bin_count - 1 :]
    quad_grad = (
        grad_cum,
        grad_end - grad_cum,
        grad_col - grad_cum,
        grad_all - grad_end - grad_col + grad_cum,
    )
    quad_hess = (
        hess_cum,
        hess_end - hess_cum,
        hess_col - hess_cum,
        hess_all - hess_end - hess_col + hess_cum,
    )
    result = -(grad_all * grad_all) / (hess_all + LAMBDA_REG)
    for grad_part, hess_part in zip(quad_grad, quad_hess):
        result = result + grad_part * grad_part / (hess_part + LAMBDA_REG)
    return result


def shards(bin_codes, gradients, hessians, pair_list, owners):
    feat_count = lax.axis_size("feat")
    row_count = lax.axis_size("row")
    feat_index = lax.axis_index("feat")
    row_index = lax.axis_index("row")
    pair_count = pair_list.shape[0]
    bin_count = BINS
    row_share = bin_count // row_count
    home_slots = 2 * pair_count // feat_count
    rank = slot_rank(owners)
    pair_ids = jnp.arange(pair_count, dtype=jnp.int32)
    places = jnp.arange(home_slots, dtype=jnp.int32)
    matched = (owners[None, :] == feat_index) & (rank[None, :] == places[:, None])
    chosen = jnp.sum(jnp.where(matched, pair_ids[None, :], 0), axis=1)
    present = jnp.any(matched, axis=1)
    lookup = owners * home_slots + rank
    chosen_pairs = pair_list[chosen]
    picked = jnp.take(bin_codes, chosen_pairs.reshape(-1), axis=0)
    picked = picked.reshape(home_slots, 2, -1)
    levels = jnp.arange(bin_count, dtype=jnp.int32)
    hot_first = (picked[:, 0, None, :] == levels[None, :, None]).astype(jnp.bfloat16)
    hot_second = (picked[:, 1, None, :] == levels[None, :, None]).astype(jnp.bfloat16)
    weighted = jnp.concatenate(
        [hot_second * gradients[None, None, :], hot_second * hessians[None, None, :]], axis=1
    )
    histogram = jnp.einsum("sar,sxr->sax", hot_first, weighted, preferred_element_type=jnp.float32)
    histogram = histogram * present[:, None, None].astype(jnp.float32)
    summed = lax.psum(histogram, "row")
    running = cumulate(summed)
    cut_rows = lax.dynamic_slice_in_dim(running, row_index * row_share, row_share, 1)
    margin_row = running[:, -1, :]
    cut_gain = cut_gains(cut_rows, margin_row).reshape(home_slots, row_share * bin_count)
    row_peak = lax.pmax(jnp.max(cut_gain, axis=1), "row")
    everyone = lax.all_gather(row_peak, "feat", axis=0, tiled=True)
    best_gain = everyone[lookup]
    return (cut_gain, best_gain)


def solution(mesh):
    in_specs = (P(None, "row"), P("row"), P("row"), P(), P())
    out_specs = (P("feat", "row"), P())
    return jax.shard_map(shards, mesh=mesh, in_specs=in_specs, out_specs=out_specs, check_vma=False)
```

profile of v0, /device:TPU:1, one launch (start us, length us, event | category | flops | bytes accessed | tf_op | source)
XLA Modules:
  0.0 291.0 jit_solution(3564876768124046581)
XLA Ops:
  7.2 0.0 copy-start
  7.2 0.0 copy-start.1
  7.2 0.0 all-reduce.3.cloned.1.call-start
  7.2 0.9 convert_reduce_fusion
  8.1 0.7 broadcast_compare_fusion
  8.8 0.1 select_reduce_fusion
  9.0 0.8 copy.58
  9.7 0.6 gather_fusion
  10.3 0.1 reshape.114
  10.4 0.1 fusion.23
  10.5 4.7 %gather_fusion.1 = s32[32,8192]{1,0:T(8,128)S(1)} fusion(s32[256,8192]{1,0:T(8,128)} %param.5, s32[1024]{0:T(1024)S(1)} %pad_clamp_fusion.1), kind=kCustom, calls=%fused_computation.1 | custom fusion | bytes 2097280 | tf_op jit(solution)/shard_map/jit(_take)/gather | solution.py:70
  15.3 0.6 gather.14
  15.9 0.1 copy.59
  16.0 0.7 copy_select_fusion
  16.7 0.1 slice_bitcast_fusion.1
  16.8 0.0 copy-done
  16.8 0.0 copy-done.1
  16.8 9.2 %fusion.5 = (bf16[16,32,8192]{2,1,0:T(8,128)(2,1)}, bf16[16,32,8192]{2,1,0:T(8,128)(2,1)}) fusion(s32[16,8192]{1,0:T(8,128)S(1)} %get-tuple-element.11, bf16[8192]{0:T(1024)(128)(2,1)S(1)} %copy-done, bf16[8192]{0:T(1024)(128)(2,1)S(1)} %copy-done.1), kind=kLoop, calls=%fused_computation.9 | loop fusion | flops 12582912 | bytes 17334272 | tf_op jit(solution)/shard_map/mul | solution.py:76
  26.0 0.0 copy-start.2
  26.0 0.0 copy-start.3
  26.0 8.4 %fusion.7 = f32[16,32,64]{2,1,0:T(8,128)S(1)} fusion(bf16[16,32,8192]{2,1,0:T(8,128)(2,1)} %get-tuple-element.13, bf16[16,32,8192]{2,1,0:T(8,128)(2,1)} %get-tuple-element.12, s32[16,8192]{1,0:T(8,128)S(1)} %get-tuple-element.10, f32[16]{0:T(128)S(1)} %convert_element_type.14), kind=kOutput, calls=%fused_computation.12 | convolution fusion | flops 574652416 | bytes 17432640 | tf_op jit(solution)/shard_map/sar,sxr->sax/dot_general | solution.py:78
  34.3 0.3 reduce_window_sum.24
  34.7 1.1 copy.61
  35.8 0.0 all-reduce.3.cloned.1.call-update
  35.8 0.0 copy-done.2
  35.8 0.0 copy-done.3
  35.8 0.6 dynamic-slice
  37.1 146.9 %all-reduce.3.cloned.1.call-done = f32[16,32,2,32]{3,0,1,2:T(8,128)} async-done(((f32[16,32,2,32]{3,0,1,2:T(8,128)}), f32[16,32,2,32]{3,0,1,2:T(8,128)}) %all-reduce.3.cloned.1.call-update) | async-done | bytes 131088 | tf_op jit(solution)/shard_map/psum | solution.py:80
  184.0 1.1 fusion.29
  185.1 0.2 copy.62
  185.2 6.1 %reduce_window_sum.26 = f32[16,32,2,32]{3,1,2,0:T(8,128)S(1)} reduce-window(f32[16,32,2,32]{3,1,2,0:T(8,128)S(1)} %copy.62, f32[]{:T(128)} %constant.45.clone.1), window={size=1x1x1x32 pad=0_0x0_0x0_0x31_0}, to_apply=%region_5.6 | reduce-window | flops 1015808 | bytes 262148 | tf_op jit(solution)/shard_map/jit(cumsum)/reduce_window_sum | solution.py:21
  191.4 0.4 copy.68
  191.8 0.3 reshape.147
  192.1 0.2 fusion.21
  192.3 0.2 fusion.16
  192.5 0.8 fusion.27
  193.3 58.4 %pmax.7 = f32[16]{0:T(128)S(1)} all-reduce(f32[16]{0:T(128)S(1)} %get-tuple-element.8), channel_id=1, replica_groups=mesh['row'=32,'feat'=8] {'row'}, use_global_device_ids=true, to_apply=%region_7.8 | all-reduce | flops 16 | bytes 128 | tf_op jit(solution)/shard_map/pmax | solution.py:85
  251.8 0.2 dynamic-update-slice
  252.0 30.9 %all-reduce = f32[128]{0:T(128)S(1)} all-reduce(f32[128]{0:T(128)S(1)} %dynamic-update-slice), channel_id=1, replica_groups=mesh['row'=32,'feat'=8] {'feat'}, use_global_device_ids=true, to_apply=%add | all-reduce | flops 128 | bytes 1024
  282.9 1.3 gather_fusion.2
  (10 shorter events, 0.1 us)
Async XLA Ops:
  7.2 9.6 %copy-start = (bf16[8192]{0:T(1024)(128)(2,1)S(1)}, bf16[8192]{0:T(1024)(128)(2,1)}, u32[]{:S(2)}) copy-start(bf16[8192]{0:T(1024)(128)(2,1)} %param.6) | copy-start | bytes 49156
  7.2 9.6 %copy-start.1 = (bf16[8192]{0:T(1024)(128)(2,1)S(1)}, bf16[8192]{0:T(1024)(128)(2,1)}, u32[]{:S(2)}) copy-start(bf16[8192]{0:T(1024)(128)(2,1)} %param.7) | copy-start | bytes 49156
  7.2 176.8 %all-reduce.3.cloned.1.call-start = ((), (), s32[]{:S(2)}) async-start(), calls=%async_computation | async-start | bytes 1048576 | tf_op jit(solution)/shard_map/psum | solution.py:80
  26.0 9.8 %copy-start.2 = (s32[64]{0:T(128)S(1)}, s32[64]{0:T(128)}, u32[]{:S(2)}) copy-start(s32[64]{0:T(128)} %param.9) | copy-start | bytes 772
  26.0 9.9 %copy-start.3 = (u32[256]{0:T(256)S(1)}, u32[256]{0:T(256)}, u32[]{:S(2)}) copy-start(u32[256]{0:T(256)} %constant.55) | copy-start | bytes 3076
Sparse Core Ops, SparseCore 0:
  35.9 148.0 all-reduce.2
where the time goes:
time: 291 us
  waiting for transfers between devices  147 us (51%)
  blocking collectives  89.3 us (31%)
  other arithmetic  20.2 us (7%)
  between operations  14.9 us (5%)
  local copies, waits for them, and re-layouts  11.4 us (4%)
  matrix products  8.35 us (3%)
    psum x1, waiting for transfers between devices, shards(): summed = lax.psum(histogram, 'row')  147 us
    pmax x1, blocking collectives, shards(): row_peak = lax.pmax(jnp.max(cut_gain, axis=1), 'row')  58.4 us
    unnamed x1, blocking collectives  30.9 us
    mul x1, other arithmetic, shards(): hot_second * gradients[None, None, :]  9.18 us
    dot_general x1, matrix products, shards(): jnp.einsum('sar,sxr->sax', hot_first, weighted, preferred_element_type=jn...  8.35 us
    another operation x1, other arithmetic, cumulate(): shaped = jnp.cumsum(shaped, axis=-1)  6.13 us
  transfers between devices with their start and end apart: 1, of which 1 were waited for; matrix products, arithmetic and copies ran while one was open for 0% of the time, Pallas kernels for 0%

commit v1 on v0

--- a/solution.py
+++ b/solution.py
@@ -5,6 +5,12 @@
 
 BINS = 32
 LAMBDA_REG = 1.0
+
+
+def summed_here(block, name):
+    terms = lax.all_gather(block, name, axis=0, tiled=False)
+    total = terms.sum(axis=0)
+    return total
 
 
 def slot_rank(owners):
@@ -77,7 +83,7 @@
     )
     histogram = jnp.einsum("sar,sxr->sax", hot_first, weighted, preferred_element_type=jnp.float32)
     histogram = histogram * present[:, None, None].astype(jnp.float32)
-    summed = lax.psum(histogram, "row")
+    summed = summed_here(histogram, "row")
     running = cumulate(summed)
     cut_rows = lax.dynamic_slice_in_dim(running, row_index * row_share, row_share, 1)
     margin_row = running[:, -1, :]

time: 291 us -> 243 us (0.84)
  waiting for transfers between devices: 147 us -> 99.8 us
  blocking collectives: 89.3 us -> 84.4 us
  other arithmetic: 20.2 us -> 23.9 us
    psum x1 -> x0, waiting for transfers between devices: 147 us -> none  [shards(): summed = lax.psum(histogram, 'row')]
    all_gather x0 -> x1, waiting for transfers between devices: none -> 99.7 us  [summed_here(): terms = lax.all_gather(block, name, axis=0, tiled=False)]
    reduce_sum x0 -> x1, other arithmetic: none -> 4.46 us  [summed_here(): total = terms.sum(axis=0)]
    unnamed x1, blocking collectives: 30.9 us -> 27.3 us
where the time goes in v1:
time: 243 us; the launch traced here: 242 us
  waiting for transfers between devices  99.8 us (41%)
  blocking collectives  84.4 us (35%)
  other arithmetic  23.9 us (10%)
  between operations  14.9 us (6%)
  local copies, waits for them, and re-layouts  10.3 us (4%)
  matrix products  9.1 us (4%)
    all_gather x1, waiting for transfers between devices, summed_here(): terms = lax.all_gather(block, name, axis=0, tiled=False)  99.7 us
    pmax x1, blocking collectives, shards(): row_peak = lax.pmax(jnp.max(cut_gain, axis=1), 'row')  57.1 us
    unnamed x1, blocking collectives  27.3 us
    mul x1, other arithmetic, shards(): hot_second * gradients[None, None, :]  9.18 us
    dot_general x1, matrix products, shards(): jnp.einsum('sar,sxr->sax', hot_first, weighted, preferred_element_type=jn...  9.1 us
    another operation x1, other arithmetic, cumulate(): shaped = jnp.cumsum(shaped, axis=-1)  6.13 us
    gather x2, local copies, waits for them, and re-layouts, shards(): picked = jnp.take(bin_codes, chosen_pairs.reshape(-1), axis=0)  5.36 us
  transfers between devices with their start and end apart: 1, of which 1 were waited for; matrix products, arithmetic and copies ran while one was open for 0% of the time, Pallas kernels for 0%

profile of v1, /device:TPU:1, one launch (start us, length us, event | category | flops | bytes accessed | tf_op | source)
XLA Modules:
  0.0 242.3 jit_solution(18271233300120912534)
XLA Ops:
  7.2 0.0 copy-start
  7.2 0.0 copy-start.1
  7.2 0.0 all-gather.3.cloned.1.call-start
  7.2 0.9 convert_reduce_fusion
  8.1 0.7 broadcast_compare_fusion
  8.8 0.1 select_reduce_fusion
  9.0 0.8 copy.72
  9.7 0.6 gather_fusion
  10.3 0.1 reshape.114
  10.4 0.1 fusion.25
  10.5 4.7 %gather_fusion.1 = s32[32,8192]{1,0:T(8,128)S(1)} fusion(s32[256,8192]{1,0:T(8,128)} %param.5, s32[1024]{0:T(1024)S(1)} %pad_clamp_fusion.1), kind=kCustom, calls=%fused_computation.1 | custom fusion | bytes 2097280 | tf_op jit(solution)/shard_map/jit(_take)/gather | solution.py:76
  15.3 0.6 gather.14
  15.9 0.1 copy.73
  16.0 0.7 copy_select_fusion
  16.7 0.1 slice_bitcast_fusion.1
  16.8 0.0 copy-done
  16.8 0.0 copy-done.1
  16.8 9.2 %fusion.5 = (bf16[16,32,8192]{2,1,0:T(8,128)(2,1)}, bf16[16,32,8192]{2,1,0:T(8,128)(2,1)}) fusion(s32[16,8192]{1,0:T(8,128)S(1)} %get-tuple-element.11, bf16[8192]{0:T(1024)(128)(2,1)S(1)} %copy-done, bf16[8192]{0:T(1024)(128)(2,1)S(1)} %copy-done.1), kind=kLoop, calls=%fused_computation.9 | loop fusion | flops 12582912 | bytes 17334272 | tf_op jit(solution)/shard_map/mul | solution.py:82
  26.0 0.0 copy-start.3
  26.0 0.0 copy-start.2
  26.0 9.1 %fusion.7 = f32[16,32,64]{2,1,0:T(8,128)} fusion(bf16[16,32,8192]{2,1,0:T(8,128)(2,1)} %get-tuple-element.13, bf16[16,32,8192]{2,1,0:T(8,128)(2,1)} %get-tuple-element.12, s32[16,8192]{1,0:T(8,128)S(1)} %get-tuple-element.10, f32[16]{0:T(128)S(1)} %convert_element_type.14), kind=kOutput, calls=%fused_computation.12 | convolution fusion | flops 574652416 | bytes 17432640 | tf_op jit(solution)/shard_map/sar,sxr->sax/dot_general | solution.py:84
  35.1 0.0 all-gather.3.cloned.1.call-update
  35.1 0.0 copy-done.3
  35.1 0.6 dynamic-slice
  36.3 0.0 copy-done.2
  36.4 99.7 %all-gather.3.cloned.1.call-done = f32[512,32,64]{2,1,0:T(8,128)} async-done(((f32[16,32,64]{2,1,0:T(8,128)}), f32[512,32,64]{2,1,0:T(8,128)}) %all-gather.3.cloned.1.call-update) | async-done | bytes 4194320 | tf_op jit(solution)/shard_map/all_gather | solution.py:11
  136.1 4.5 %reduce_sum.32 = f32[16,32,64]{2,1,0:T(8,128)S(1)} reduce(f32[32,16,32,64]{3,2,1,0:T(8,128)} %bitcast.59, f32[]{:T(128)} %constant.46.clone.1), dimensions={0}, to_apply=%region_3.4 | reduce | flops 1015808 | bytes 4325380 | tf_op jit(solution)/shard_map/reduce_sum | solution.py:12
  140.6 0.3 reduce_window_sum.24
  140.9 0.4 fusion.10
  141.3 0.2 copy.76
  141.5 6.1 %reduce_window_sum.26 = f32[16,32,2,32]{3,1,2,0:T(8,128)S(1)} reduce-window(f32[16,32,2,32]{3,1,2,0:T(8,128)S(1)} %copy.76, f32[]{:T(128)} %constant.46.clone.1), window={size=1x1x1x32 pad=0_0x0_0x0_0x31_0}, to_apply=%region_5.6 | reduce-window | flops 1015808 | bytes 262148 | tf_op jit(solution)/shard_map/jit(cumsum)/reduce_window_sum | solution.py:27
  147.6 0.4 copy.82
  148.0 0.3 reshape.148
  148.3 0.2 fusion.23
  148.5 0.2 fusion.18
  148.8 0.8 fusion.29
  149.6 57.1 %pmax.7 = f32[16]{0:T(128)S(1)} all-reduce(f32[16]{0:T(128)S(1)} %get-tuple-element.8), channel_id=1, replica_groups=mesh['row'=32,'feat'=8] {'row'}, use_global_device_ids=true, to_apply=%region_7.8 | all-reduce | flops 16 | bytes 128 | tf_op jit(solution)/shard_map/pmax | solution.py:91
  206.6 0.2 dynamic-update-slice
  206.9 27.3 %all-reduce = f32[128]{0:T(128)S(1)} all-reduce(f32[128]{0:T(128)S(1)} %dynamic-update-slice), channel_id=1, replica_groups=mesh['row'=32,'feat'=8] {'feat'}, use_global_device_ids=true, to_apply=%add | all-reduce | flops 128 | bytes 1024
  234.2 1.3 gather_fusion.2
  (10 shorter events, 0.1 us)
Async XLA Ops:
  7.2 9.6 %copy-start = (bf16[8192]{0:T(1024)(128)(2,1)S(1)}, bf16[8192]{0:T(1024)(128)(2,1)}, u32[]{:S(2)}) copy-start(bf16[8192]{0:T(1024)(128)(2,1)} %param.6) | copy-start | bytes 49156
  7.2 9.6 %copy-start.1 = (bf16[8192]{0:T(1024)(128)(2,1)S(1)}, bf16[8192]{0:T(1024)(128)(2,1)}, u32[]{:S(2)}) copy-start(bf16[8192]{0:T(1024)(128)(2,1)} %param.7) | copy-start | bytes 49156
  7.2 128.9 %all-gather.3.cloned.1.call-start = ((), (), s32[]{:S(2)}) async-start(), calls=%async_computation | async-start | bytes 8650752 | tf_op jit(solution)/shard_map/all_gather | solution.py:11
  26.0 9.1 %copy-start.3 = (u32[256]{0:T(256)S(1)}, u32[256]{0:T(256)}, u32[]{:S(2)}) copy-start(u32[256]{0:T(256)} %constant.56) | copy-start | bytes 3076
  26.0 10.4 %copy-start.2 = (s32[64]{0:T(128)S(1)}, s32[64]{0:T(128)}, u32[]{:S(2)}) copy-start(s32[64]{0:T(128)} %param.9) | copy-start | bytes 772
Sparse Core Ops, SparseCore 0:
  35.2 100.8 all-gather.2
